TPU v7x, 128 devices: a whole 4x4x4 slice. The times are simulated.
128 devices in a mesh: px: 32 (over z, x, core), vx: 4 (over y).
Axes of the slice: x: 4, y: 4, z: 4, core: 2. Of those that a mesh axis runs over, the one named last changes fastest.
Arguments:
- value_field: float32 [64, 96, 64, 384], P('px', 'vx'), may hold values from -6 to 6
- cost_field: float32 [64, 96, 64, 384], P('px', 'vx'), may hold values from -6 to 6
- accel_first: float32 [64, 96], P('px', 'vx'), may hold values from -3 to 3
- accel_second: float32 [64, 384], replicated, may hold values from -1 to 1
Outputs:
- final_value: float32 [64, 96, 64, 384], P('px', 'vx')
- funnel_slice: float32 [64, 384], P('px')
All inputs are finite; a program needn't handle non-finite values.
Results may differ from a plain program's by a relative error of at most 0.00002.
Values sent between devices are 32-bit elements; how exact they have to be, the bound alone decides.
A program may use at most 128 MiB of HBM per device.

v0:
```python
import jax
import jax.numpy as jnp
from jax import lax
from jax.sharding import PartitionSpec as P

VELOCITY_LIMIT = 1.0
PLANNER_SPEED = 0.3
DISTURBANCE = 0.2
CONTROL_COST = 1.0
COURANT = 0.5


def padded_2(cells, sides, width):
    for axis, dim in sides:
        count = lax.axis_size(axis)
        ends = count - 1
        head = lax.slice_in_dim(cells, 0, width, axis=dim)
        tail = lax.slice_in_dim(cells, cells.shape[dim] - width, cells.shape[dim], axis=dim)
        cells = jnp.concatenate(
            [
                lax.ppermute(tail, axis, [(i, (i + 1) % count) for i in range(ends)]),
                cells,
                lax.ppermute(head, axis, [((i + 1) % count, i) for i in range(ends)]),
            ],
            axis=dim,
        )
    return cells


def interior(padded, dimension, offset):
    index_list = []
    for axis_number in range(4):
        size_here = padded.shape[axis_number]
        if axis_number == dimension:
            index_list.append(slice(1 + offset, size_here - 1 + offset))
        else:
            index_list.append(slice(1, size_here - 1))
    return padded[tuple(index_list)]


def slopes(padded, spacings):
    center = interior(padded, 0, 0)
    gradients = []
    curvatures = []
    for dimension in range(4):
        upper = interior(padded, dimension, 1)
        lower = interior(padded, dimension, -1)
        gradients.append((upper - lower) / (2.0 * spacings[dimension]))
        curvatures.append((upper - 2.0 * center + lower) / spacings[dimension])
    return (center, gradients, curvatures)


def hamiltonian(gradients, curvatures, speed_first, speed_second, push_first, push_second, rates):
    total = gradients[0] * speed_first + gradients[3] * speed_second
    total = total + PLANNER_SPEED * (jnp.abs(gradients[0]) + jnp.abs(gradients[3]))
    total = total + gradients[1] * push_first + gradients[2] * push_second
    total = total + DISTURBANCE * (jnp.abs(gradients[1]) + jnp.abs(gradients[2]))
    total = total - (gradients[1] * gradients[1] + gradients[2] * gradients[2]) / (
        2.0 * CONTROL_COST
    )
    damping = (
        rates[0] * curvatures[0]
        + rates[1] * curvatures[1]
        + rates[2] * curvatures[2]
        + rates[3] * curvatures[3]
    )
    return total - 0.5 * damping


def fill_edges(padded, width):
    edge_flags = (
        (0, lax.axis_index("px") == 0, lax.axis_index("px") == lax.axis_size("px") - 1),
        (1, lax.axis_index("vx") == 0, lax.axis_index("vx") == lax.axis_size("vx") - 1),
    )
    for dimension, is_first, is_last in edge_flags:
        count = padded.shape[dimension]
        low_edge = lax.slice_in_dim(padded, width, width + 1, axis=dimension)
        high_edge = lax.slice_in_dim(padded, count - width - 1, count - width, axis=dimension)
        shape_small = [1, 1, 1, 1]
        shape_small[dimension] = count
        position = lax.broadcasted_iota(jnp.int32, tuple(shape_small), dimension)
        padded = jnp.where(jnp.logical_and(is_first, position < width), low_edge, padded)
        padded = jnp.where(jnp.logical_and(is_last, position >= count - width), high_edge, padded)
    return padded


def pad_local(padded):
    return jnp.pad(padded, ((0, 0), (0, 0), (1, 1), (1, 1)), mode="edge")


def halo_once(field):
    return padded_2(field, (("px", 0), ("vx", 1)), 1)


def bound_speeds(gradient_vx, gradient_vy):
    return lax.pmax((jnp.max(jnp.abs(gradient_vx)), jnp.max(jnp.abs(gradient_vy))), ("px", "vx"))


def per_device(value_field, cost_field, accel_first, accel_second):
    cells_x = value_field.shape[0]
    cells_v = value_field.shape[1]
    total_vx = cells_v * lax.axis_size("vx")
    total_vy = value_field.shape[2]
    velocity_step_x = 2.0 * VELOCITY_LIMIT / total_vx
    velocity_step_y = 2.0 * VELOCITY_LIMIT / total_vy
    position_step = velocity_step_x * velocity_step_y
    spacings = (position_step, velocity_step_x, velocity_step_y, position_step)
    first_global = lax.axis_index("vx") * cells_v
    speed_second = (
        (2.0 * jnp.arange(total_vy, dtype=jnp.float32) + 1.0 - total_vy)
        * (VELOCITY_LIMIT / total_vy)
    ).reshape(total_vy, 1)
    push_limit = lax.pmax(jnp.max(jnp.abs(accel_first)), ("px", "vx"))
    push_second_limit = jnp.max(jnp.abs(accel_second))
    rate_first = VELOCITY_LIMIT * (total_vx - 1) / total_vx + PLANNER_SPEED
    rate_last = VELOCITY_LIMIT * (total_vy - 1) / total_vy + PLANNER_SPEED

    def make_rates(maxima):
        return (
            rate_first,
            push_limit + DISTURBANCE + maxima[0] / CONTROL_COST,
            push_second_limit + DISTURBANCE + maxima[1] / CONTROL_COST,
            rate_last,
        )

    positions = (first_global + jnp.arange(cells_v, dtype=jnp.int32)).astype(jnp.float32)
    speed_own = ((2.0 * positions + 1.0 - total_vx) * (VELOCITY_LIMIT / total_vx)).reshape(
        cells_v, 1, 1
    )
    push_own = accel_first.reshape(cells_x, cells_v, 1, 1)
    current = value_field
    for repeat in range(2):
        padded = pad_local(fill_edges(halo_once(current), 1))
        center, gradients, curvatures = slopes(padded, spacings)
        rates = make_rates(bound_speeds(gradients[1], gradients[2]))
        step_size = COURANT / (
            rates[0] / spacings[0]
            + rates[1] / spacings[1]
            + rates[2] / spacings[2]
            + rates[3] / spacings[3]
        )
        change = hamiltonian(
            gradients, curvatures, speed_own, speed_second, push_own, accel_second, rates
        )
        middle = jnp.maximum(cost_field, center + step_size * change)
        padded = pad_local(fill_edges(halo_once(middle), 1))
        center, gradients, curvatures = slopes(padded, spacings)
        rates = make_rates(bound_speeds(gradients[1], gradients[2]))
        change = hamiltonian(
            gradients, curvatures, speed_own, speed_second, push_own, accel_second, rates
        )
        current = jnp.maximum(cost_field, 0.5 * current + 0.5 * (center + step_size * change))
    funnel_local = jnp.min(current, axis=(1, 2))
    funnel_slice = lax.pmin(funnel_local, "vx")
    return (current, funnel_slice)


def solution(mesh):
    placed = (P("px", "vx", None, None), P("px", "vx", None, None), P("px", "vx"), P())
    return jax.shard_map(
        per_device,
        mesh=mesh,
        in_specs=placed,
        out_specs=(P("px", "vx", None, None), P("px", None)),
        check_vma=False,
    )
```

profile of v0, /device:TPU:1, one launch (start us, length us, event | category | flops | bytes accessed | tf_op | source)
XLA Modules:
  0.0 634.9 jit_solution(2219874885403228045)
XLA Ops:
  0.6 5.1 fusion.55
  5.8 4.5 collective-permute-start
  13.5 22.8 %collective-permute-done = f32[1,24,64,384]{3,2,1,0:T(8,128)} collective-permute-done((f32[1,24,64,384]{3,2,1,0:T(8,128)}, f32[1,24,64,384]{3,2,1,0:T(8,128)}, u32[]{:S(2)}, u32[]{:S(2)}) %collective-permute-start) | collective-permute-done | bytes 2359328 | tf_op jit(solution)/shard_map/ppermute | solution.py:21
  38.5 2.1 collective-permute-done.1
  41.0 3.2 collective-permute-start.2
  46.2 2.7 collective-permute-done.2
  48.9 3.8 collective-permute-done.3
  52.7 4.6 pad_maximum_fusion
  57.3 2.8 slice_bitcast_fusion.7
  60.2 2.0 select_select_fusion.7
  62.3 4.9 select_select_fusion.6
  67.4 4.7 abs_reduce_fusion.7
  72.1 70.4 %all-reduce.3 = (f32[]{:T(128)}, f32[]{:T(128)}, f32[]{:T(128)}) all-reduce(f32[]{:T(128)} %get-tuple-element.9, f32[]{:T(128)} %get-tuple-element.64, f32[]{:T(128)} %get-tuple-element.8), channel_id=1, replica_groups=mesh['px'=32,'vx'=4] {'px','vx'}, use_global_device_ids=true, to_apply=%region_6.7 | all-reduce | flops 3 | bytes 24 | tf_op jit(solution)/shard_map/pmax | solution.py:96
  144.4 24.4 %add_maximum_fusion.1 = f32[2,24,64,384]{3,2,1,0:T(8,128)S(1)} fusion(f32[2,24,64,384]{3,2,1,0:T(8,128)} %param.5, f32[4,26,64,384]{3,2,1,0:T(8,128)} %copy-done.1, f32[4,26,1,384]{3,2,1,0:T(1,128)S(1)} %get-tuple-element.40, f32[4,26,1,384]{3,2,1,0:T(1,128)S(1)} %get-tuple-element.39, f32[]{:T(128)S(6)} %div.105, f32[]{:T(128)S(6)} %div.103, ...), kind=kLoop, calls=%fused_computation.104 | loop fusion | flops 86114304 | bytes 43672108 | tf_op jit(solution)/shard_map/max | solution.py:145
  169.3 3.7 collective-permute-start.4
  173.0 1.9 collective-permute-start.5
  174.9 23.8 %collective-permute-done.4 = f32[1,24,64,384]{3,2,1,0:T(8,128)S(1)} collective-permute-done((f32[1,24,64,384]{3,2,1,0:T(8,128)S(1)}, f32[1,24,64,384]{3,2,1,0:T(8,128)S(1)}, u32[]{:S(2)}, u32[]{:S(2)}) %collective-permute-start.4) | collective-permute-done | bytes 2359328 | tf_op jit(solution)/shard_map/ppermute | solution.py:21
  198.8 4.4 collective-permute-done.5
  206.2 3.4 collective-permute-done.6
  209.6 3.8 collective-permute-done.7
  214.5 3.1 select_select_fusion.5
  217.6 4.5 select_select_fusion.4
  222.4 4.7 abs_reduce_fusion.5
  227.1 68.1 %all-reduce.2 = (f32[]{:T(128)}, f32[]{:T(128)}) all-reduce(f32[]{:T(128)} %get-tuple-element.7, f32[]{:T(128)} %get-tuple-element.6), channel_id=1, replica_groups=mesh['px'=32,'vx'=4] {'px','vx'}, use_global_device_ids=true, to_apply=%region_10.11 | all-reduce | flops 2 | bytes 16 | tf_op jit(solution)/shard_map/pmax | solution.py:96
  296.5 25.3 %multiply_maximum_fusion.1 = f32[2,24,64,384]{3,2,1,0:T(8,128)S(1)} fusion(f32[2,24,64,384]{3,2,1,0:T(8,128)} %param.5, f32[2,24,64,384]{3,2,1,0:T(8,128)} %param.4, f32[4,26,64,384]{3,2,1,0:T(8,128)} %copy-done.3, f32[4,26,1,384]{3,2,1,0:T(1,128)S(1)} %get-tuple-element.34, f32[4,26,1,384]{3,2,1,0:T(1,128)S(1)} %get-tuple-element.33, f32[]{:T(128)S(6)} %mul.414, ...), kind=kLoop, calls=%fused_computation.96 | loop fusion | flops 88473600 | bytes 48390700 | tf_op jit(solution)/shard_map/max | solution.py:152
  322.3 3.3 collective-permute-start.8
  327.5 23.8 %collective-permute-done.8 = f32[1,24,64,384]{3,2,1,0:T(8,128)S(1)} collective-permute-done((f32[1,24,64,384]{3,2,1,0:T(8,128)S(1)}, f32[1,24,64,384]{3,2,1,0:T(8,128)S(1)}, u32[]{:S(2)}, u32[]{:S(2)}) %collective-permute-start.8) | collective-permute-done | bytes 2359328 | tf_op jit(solution)/shard_map/ppermute | solution.py:21
  351.3 4.4 collective-permute-done.9
  358.5 3.4 collective-permute-done.10
  361.9 3.8 collective-permute-done.11
  366.8 3.1 select_select_fusion.3
  369.9 4.5 select_select_fusion.2
  374.7 4.7 abs_reduce_fusion.3
  379.4 68.9 %all-reduce.1 = (f32[]{:T(128)}, f32[]{:T(128)}) all-reduce(f32[]{:T(128)} %get-tuple-element.5, f32[]{:T(128)} %get-tuple-element.4), channel_id=1, replica_groups=mesh['px'=32,'vx'=4] {'px','vx'}, use_global_device_ids=true, to_apply=%region_14.15 | all-reduce | flops 2 | bytes 16 | tf_op jit(solution)/shard_map/pmax | solution.py:96
  449.5 24.4 %add_maximum_fusion = f32[2,24,64,384]{3,2,1,0:T(8,128)S(1)} fusion(f32[2,24,64,384]{3,2,1,0:T(8,128)} %param.5, f32[4,26,64,384]{3,2,1,0:T(8,128)} %copy-done.2, f32[4,26,1,384]{3,2,1,0:T(1,128)S(1)} %get-tuple-element.28, f32[4,26,1,384]{3,2,1,0:T(1,128)S(1)} %get-tuple-element.27, f32[]{:T(128)S(6)} %div.118, f32[]{:T(128)S(6)} %div.116, f32[]{:T(128)S(6)} %div.119, ...), kind=kLoop, calls=%fused_computation.88 | loop fusion | flops 86114304 | bytes 43672108 | tf_op jit(solution)/shard_map/max | solution.py:145
  474.5 2.5 collective-permute-start.12
  476.9 2.0 collective-permute-start.13
  478.9 23.8 %collective-permute-done.12 = f32[1,24,64,384]{3,2,1,0:T(8,128)S(1)} collective-permute-done((f32[1,24,64,384]{3,2,1,0:T(8,128)S(1)}, f32[1,24,64,384]{3,2,1,0:T(8,128)S(1)}, u32[]{:S(2)}, u32[]{:S(2)}) %collective-permute-start.12) | collective-permute-done | bytes 2359328 | tf_op jit(solution)/shard_map/ppermute | solution.py:21
  502.7 4.4 collective-permute-done.13
  507.2 2.3 collective-permute-start.14
  510.7 3.4 collective-permute-done.14
  514.1 3.8 collective-permute-done.15
  519.1 3.1 select_select_fusion.1
  522.2 4.5 select_select_fusion
  527.0 4.7 abs_reduce_fusion.1
  531.6 68.2 %all-reduce = (f32[]{:T(128)}, f32[]{:T(128)}) all-reduce(f32[]{:T(128)} %get-tuple-element.3, f32[]{:T(128)} %get-tuple-element.2), channel_id=1, replica_groups=mesh['px'=32,'vx'=4] {'px','vx'}, use_global_device_ids=true, to_apply=%region_18.19 | all-reduce | flops 2 | bytes 16 | tf_op jit(solution)/shard_map/pmax | solution.py:96
  601.0 26.4 %fusion.46 = (f32[2,384]{1,0:T(2,128)S(1)}, f32[2,24,64,384]{3,2,1,0:T(8,128)}) fusion(f32[2,24,64,384]{3,2,1,0:T(8,128)} %param.5, f32[2,24,64,384]{3,2,1,0:T(8,128)} %copy-done.4, f32[]{:T(128)S(6)} %mul.452, f32[]{:T(128)S(6)} %mul.449, f32[64,384]{1,0:T(8,128)S(1)} %get-tuple-element.61, f32[4,26,64,384]{3,2,1,0:T(8,128)} %copy-done, ...), kind=kLoop, calls=%fused_computation.162 | loop fusion | flops 89652480 | bytes 48393772 | tf_op jit(solution)/shard_map/reduce_min | solution.py:153
  627.5 7.2 %pmin.7 = f32[2,384]{1,0:T(2,128)} all-reduce(f32[2,384]{1,0:T(2,128)S(1)} %get-tuple-element.19), channel_id=1, replica_groups=mesh['px'=32,'vx'=4] {'vx'}, use_global_device_ids=true, to_apply=%region_20.21 | all-reduce | flops 768 | bytes 6144 | tf_op jit(solution)/shard_map/pmin | solution.py:154
  (54 shorter events, 21.9 us)
Async XLA Ops:
  0.6 11.6 %copy-start.6 = (f32[64,384]{1,0:T(8,128)S(1)}, f32[64,384]{1,0:T(8,128)}, u32[]{:S(2)}) copy-start(f32[64,384]{1,0:T(8,128)} %param.7) | copy-start | bytes 294916
  5.8 30.6 %collective-permute-start = (f32[1,24,64,384]{3,2,1,0:T(8,128)}, f32[1,24,64,384]{3,2,1,0:T(8,128)}, u32[]{:S(2)}, u32[]{:S(2)}) collective-permute-start(f32[1,24,64,384]{3,2,1,0:T(8,128)} %get-tuple-element.60), channel_id=1, source_target_pairs={{0,4},{4,8},{8,12},{12,16},{16,20},{20,24},{24,28},{28,32},{32,36}... | collective-permute-start | bytes 7077896 | tf_op jit(solution)/shard_map/ppermute | solution.py:21
  10.3 30.4 %collective-permute-start.1 = (f32[1,24,64,384]{3,2,1,0:T(8,128)}, f32[1,24,64,384]{3,2,1,0:T(8,128)S(1)}, u32[]{:S(2)}, u32[]{:S(2)}) collective-permute-start(f32[1,24,64,384]{3,2,1,0:T(8,128)} %get-tuple-element.59), channel_id=1, source_target_pairs={{4,0},{8,4},{12,8},{16,12},{20,16},{24,20},{28,24},{32,28},{36,32}... | collective-permute-start | bytes 7077896 | tf_op jit(solution)/shard_map/ppermute | solution.py:23
  13.5 24.7 %copy-start.5 = (f32[2,24,64,384]{3,2,1,0:T(8,128)S(1)}, f32[2,24,64,384]{3,2,1,0:T(8,128)}, u32[]{:S(2)}) copy-start(f32[2,24,64,384]{3,2,1,0:T(8,128)} %param.4) | copy-start | bytes 14155780
  38.5 7.0 %copy-start.7 = (f32[2,24]{1,0:T(2,128)S(1)}, f32[2,24]{1,0:T(2,128)}, u32[]{:S(2)}) copy-start(f32[2,24]{1,0:T(2,128)} %param.6) | copy-start | bytes 580
  41.0 7.9 %collective-permute-start.2 = (f32[4,1,64,384]{3,2,1,0:T(8,128)S(1)}, f32[4,1,64,384]{3,2,1,0:T(8,128)S(1)}, u32[]{:S(2)}, u32[]{:S(2)}) collective-permute-start(f32[4,1,64,384]{3,2,1,0:T(8,128)S(1)} %get-tuple-element.51), channel_id=1, source_target_pairs={{0,1},{1,2},{2,3},{4,5},{5,6},{6,7},{8,9},{9,10},{10,11},{12,13},{... | collective-permute-start | bytes 1179656 | tf_op jit(solution)/shard_map/ppermute | solution.py:21
  44.2 8.5 %collective-permute-start.3 = (f32[4,1,64,384]{3,2,1,0:T(8,128)S(1)}, f32[4,1,64,384]{3,2,1,0:T(8,128)S(1)}, u32[]{:S(2)}, u32[]{:S(2)}) collective-permute-start(f32[4,1,64,384]{3,2,1,0:T(8,128)S(1)} %get-tuple-element.52), channel_id=1, source_target_pairs={{1,0},{2,1},{3,2},{5,4},{6,5},{7,6},{9,8},{10,9},{11,10},{13,12},{... | collective-permute-start | bytes 1179656 | tf_op jit(solution)/shard_map/ppermute | solution.py:23
  67.2 4.9 copy-start.1
  169.3 29.5 %collective-permute-start.4 = (f32[1,24,64,384]{3,2,1,0:T(8,128)S(1)}, f32[1,24,64,384]{3,2,1,0:T(8,128)S(1)}, u32[]{:S(2)}, u32[]{:S(2)}) collective-permute-start(f32[1,24,64,384]{3,2,1,0:T(8,128)S(1)} %get-tuple-element.57), channel_id=1, source_target_pairs={{0,4},{4,8},{8,12},{12,16},{16,20},{20,24},{24,28},{28,32},{32,36}... | collective-permute-start | bytes 7077896 | tf_op jit(solution)/shard_map/ppermute | solution.py:21
  173.0 30.2 %collective-permute-start.5 = (f32[1,24,64,384]{3,2,1,0:T(8,128)S(1)}, f32[1,24,64,384]{3,2,1,0:T(8,128)S(1)}, u32[]{:S(2)}, u32[]{:S(2)}) collective-permute-start(f32[1,24,64,384]{3,2,1,0:T(8,128)S(1)} %get-tuple-element.58), channel_id=1, source_target_pairs={{4,0},{8,4},{12,8},{16,12},{20,16},{24,20},{28,24},{32,28},{36,32}... | collective-permute-start | bytes 7077896 | tf_op jit(solution)/shard_map/ppermute | solution.py:23
  203.2 6.3 collective-permute-start.6
  204.9 8.5 %collective-permute-start.7 = (f32[4,1,64,384]{3,2,1,0:T(8,128)S(1)}, f32[4,1,64,384]{3,2,1,0:T(8,128)S(1)}, u32[]{:S(2)}, u32[]{:S(2)}) collective-permute-start(f32[4,1,64,384]{3,2,1,0:T(8,128)S(1)} %get-tuple-element.50), channel_id=1, source_target_pairs={{1,0},{2,1},{3,2},{5,4},{6,5},{7,6},{9,8},{10,9},{11,10},{13,12},{... | collective-permute-start | bytes 1179656 | tf_op jit(solution)/shard_map/ppermute | solution.py:23
  222.2 4.9 copy-start.3
  321.8 48.2 %copy-start.4 = (f32[2,24,64,384]{3,2,1,0:T(8,128)}, f32[2,24,64,384]{3,2,1,0:T(8,128)S(1)}, u32[]{:S(2)}) copy-start(f32[2,24,64,384]{3,2,1,0:T(8,128)S(1)} %multiply_maximum_fusion.1) | copy-start | bytes 14155780
  322.3 29.0 %collective-permute-start.8 = (f32[1,24,64,384]{3,2,1,0:T(8,128)S(1)}, f32[1,24,64,384]{3,2,1,0:T(8,128)S(1)}, u32[]{:S(2)}, u32[]{:S(2)}) collective-permute-start(f32[1,24,64,384]{3,2,1,0:T(8,128)S(1)} %get-tuple-element.55), channel_id=1, source_target_pairs={{0,4},{4,8},{8,12},{12,16},{16,20},{20,24},{24,28},{28,32},{32,36}... | collective-permute-start | bytes 7077896 | tf_op jit(solution)/shard_map/ppermute | solution.py:21
  325.6 30.2 %collective-permute-start.9 = (f32[1,24,64,384]{3,2,1,0:T(8,128)S(1)}, f32[1,24,64,384]{3,2,1,0:T(8,128)S(1)}, u32[]{:S(2)}, u32[]{:S(2)}) collective-permute-start(f32[1,24,64,384]{3,2,1,0:T(8,128)S(1)} %get-tuple-element.56), channel_id=1, source_target_pairs={{4,0},{8,4},{12,8},{16,12},{20,16},{24,20},{28,24},{32,28},{36,32}... | collective-permute-start | bytes 7077896 | tf_op jit(solution)/shard_map/ppermute | solution.py:23
  355.8 6.1 collective-permute-start.10
  357.2 8.5 %collective-permute-start.11 = (f32[4,1,64,384]{3,2,1,0:T(8,128)S(1)}, f32[4,1,64,384]{3,2,1,0:T(8,128)S(1)}, u32[]{:S(2)}, u32[]{:S(2)}) collective-permute-start(f32[4,1,64,384]{3,2,1,0:T(8,128)S(1)} %get-tuple-element.48), channel_id=1, source_target_pairs={{1,0},{2,1},{3,2},{5,4},{6,5},{7,6},{9,8},{10,9},{11,10},{13,12},{... | collective-permute-start | bytes 1179656 | tf_op jit(solution)/shard_map/ppermute | solution.py:23
  374.5 4.9 copy-start.2
  474.5 28.2 %collective-permute-start.12 = (f32[1,24,64,384]{3,2,1,0:T(8,128)S(1)}, f32[1,24,64,384]{3,2,1,0:T(8,128)S(1)}, u32[]{:S(2)}, u32[]{:S(2)}) collective-permute-start(f32[1,24,64,384]{3,2,1,0:T(8,128)S(1)} %get-tuple-element.53), channel_id=1, source_target_pairs={{0,4},{4,8},{8,12},{12,16},{16,20},{20,24},{24,28},{28,32},{32,36}... | collective-permute-start | bytes 7077896 | tf_op jit(solution)/shard_map/ppermute | solution.py:21
  476.9 30.2 %collective-permute-start.13 = (f32[1,24,64,384]{3,2,1,0:T(8,128)S(1)}, f32[1,24,64,384]{3,2,1,0:T(8,128)S(1)}, u32[]{:S(2)}, u32[]{:S(2)}) collective-permute-start(f32[1,24,64,384]{3,2,1,0:T(8,128)S(1)} %get-tuple-element.54), channel_id=1, source_target_pairs={{4,0},{8,4},{12,8},{16,12},{20,16},{24,20},{28,24},{32,28},{36,32}... | collective-permute-start | bytes 7077896 | tf_op jit(solution)/shard_map/ppermute | solution.py:23
  507.2 7.0 %collective-permute-start.14 = (f32[4,1,64,384]{3,2,1,0:T(8,128)S(1)}, f32[4,1,64,384]{3,2,1,0:T(8,128)S(1)}, u32[]{:S(2)}, u32[]{:S(2)}) collective-permute-start(f32[4,1,64,384]{3,2,1,0:T(8,128)S(1)} %get-tuple-element.45), channel_id=1, source_target_pairs={{0,1},{1,2},{2,3},{4,5},{5,6},{6,7},{8,9},{9,10},{10,11},{12,13},{... | collective-permute-start | bytes 1179656 | tf_op jit(solution)/shard_map/ppermute | solution.py:21
  509.4 8.5 %collective-permute-start.15 = (f32[4,1,64,384]{3,2,1,0:T(8,128)S(1)}, f32[4,1,64,384]{3,2,1,0:T(8,128)S(1)}, u32[]{:S(2)}, u32[]{:S(2)}) collective-permute-start(f32[4,1,64,384]{3,2,1,0:T(8,128)S(1)} %get-tuple-element.46), channel_id=1, source_target_pairs={{1,0},{2,1},{3,2},{5,4},{6,5},{7,6},{9,8},{10,9},{11,10},{13,12},{... | collective-permute-start | bytes 1179656 | tf_op jit(solution)/shard_map/ppermute | solution.py:23
  526.7 4.9 copy-start
where the time goes:
time: 643 us; the launch traced here: 635 us
  blocking collectives  283 us (44%)
  other arithmetic  157 us (24%)
  waiting for transfers between devices  138 us (21%)
  starting transfers between devices  35.4 us (6%)
  local copies, waits for them, and re-layouts  14.1 us (2%)
  between operations  7.74 us (1%)
    pmax x4, blocking collectives, bound_speeds(): lax.pmax((jnp.max(jnp.abs(gradient_vx)), jnp.max(jnp.abs(gradient_vy))),...  275 us
    ppermute x8, waiting for transfers between devices, padded_2(): lax.ppermute(tail, axis, [(i, (i + 1) % count) for i in range(ends)])  107 us
    max x2, other arithmetic, per_device(): middle = jnp.maximum(cost_field, center + step_size * change)  48.8 us
    ppermute x8, waiting for transfers between devices, padded_2(): lax.ppermute(head, axis, [((i + 1) % count, i) for i in range(ends)])  30.7 us
    select_n x8, other arithmetic, fill_edges(): jnp.where(jnp.logical_and(is_last, position >= count - width), high_edge,...  29.7 us
    reduce_min x1, other arithmetic, per_device(): funnel_local = jnp.min(current, axis=(1, 2))  26.4 us
    max x1, other arithmetic, per_device(): jnp.maximum(cost_field, 0.5 * current + 0.5 * (center + step_size * change))  25.3 us
    ppermute x8, starting transfers between devices, padded_2(): lax.ppermute(tail, axis, [(i, (i + 1) % count) for i in range(ends)])  22.4 us
  transfers between devices with their start and end apart: 16, of which 16 were waited for; matrix products, arithmetic and copies ran while one was open for 1% of the time, Pallas kernels for 0%

commit v1 on v0

v1 whole, which is shorter than its diff:
```python
import functools

import jax
import jax.numpy as jnp
from jax import lax
from jax.experimental import pallas as pl
from jax.experimental.pallas import tpu as pltpu
from jax.sharding import PartitionSpec as P

MESH = pl.DeviceIdType.MESH
VELOCITY_LIMIT = 1.0
PLANNER_SPEED = 0.3
DISTURBANCE = 0.2
CONTROL_COST = 1.0
COURANT = 0.5
CHUNK = 1
RING = 4


def kernel(
    a1_s,
    a1_v,
    value,
    cost_hbm,
    a2_hbm,
    out,
    funnel,
    f0,
    f1,
    f2,
    f3,
    cost,
    a2,
    tab_v,
    tab_a,
    red_s,
    red_r,
    coef,
    fun_s,
    fun_r,
    px_send,
    px_recv,
    vx_send,
    vx_recv,
    red_send,
    red_recv,
    fun_send,
    fun_recv,
    load_sem,
):
    fields = (f0, f1, f2, f3)
    rows = cost.shape[1]
    tall = cost.shape[2]
    wide = cost.shape[3]
    strips = tall // 8
    tiles = wide // 128
    chunks = rows // CHUNK
    px, vx = lax.axis_index("px"), lax.axis_index("vx")
    npx, nvx = lax.axis_size("px"), lax.axis_size("vx")
    total_vx = rows * nvx
    h2 = 2.0 * VELOCITY_LIMIT / total_vx
    h3 = 2.0 * VELOCITY_LIMIT / tall
    h1 = h2 * h3
    r1 = VELOCITY_LIMIT * (total_vx - 1) / total_vx + PLANNER_SPEED
    r4 = VELOCITY_LIMIT * (tall - 1) / tall + PLANNER_SPEED

    core = px % 2
    chip_x = (px // 2) % RING
    chip_z = px // (2 * RING)
    has_left, has_right = px > 0, px < npx - 1
    has_down, has_up = vx > 0, vx < nvx - 1
    first_p = (npx - 1 - px) // (npx - 1)
    last_p = px // (npx - 1)
    first_v = (nvx - 1 - vx) // (nvx - 1)
    last_v = vx // (nvx - 1)
    plane_low = first_p
    plane_high = 3 - last_p

    def ring_device(axis, step, which):
        if axis == "z":
            return (((chip_z + step) % RING * RING + chip_x) * 2 + which, vx)
        if axis == "x":
            return ((chip_z * RING + (chip_x + step) % RING) * 2 + which, vx)
        return ((chip_z * RING + chip_x) * 2 + which, (vx + step) % RING)

    partner = (px + 1 - 2 * core, vx)

    load_value = pltpu.make_async_copy(
        value, f0.at[pl.ds(1, 2), pl.ds(1, rows)], load_sem.at[0]
    )
    load_cost = pltpu.make_async_copy(cost_hbm, cost, load_sem.at[1])
    load_a2 = pltpu.make_async_copy(a2_hbm, a2, load_sem.at[2])
    load_value.start()

    barrier = pltpu.get_barrier_semaphore()

    def greet(device):
        pl.semaphore_signal(barrier, inc=1, device_id=device, device_id_type=MESH)

    greet(partner)
    for axis in ("x", "y", "z"):
        for step in range(1, RING):
            for which in (0, 1):
                greet(ring_device(axis, step, which))
    far_left = jnp.logical_and(jnp.logical_and(core == 0, chip_x == 0), has_left)
    far_right = jnp.logical_and(
        jnp.logical_and(core == 1, chip_x == RING - 1), has_right
    )

    @pl.when(far_left)
    def _():
        greet((px - 1, vx))

    @pl.when(far_right)
    def _():
        greet((px + 1, vx))

    far = far_left.astype(jnp.int32) + far_right.astype(jnp.int32)
    pl.semaphore_wait(barrier, 1 + 3 * 2 * (RING - 1) + far)

    def px_copy(stage, side, chunk):
        dst_plane = 3 if side == 0 else 0
        span = pl.ds(chunk * CHUNK + 1, CHUNK)
        if stage == 0:
            src = value.at[side, pl.ds(chunk * CHUNK, CHUNK)]
        else:
            src = fields[stage].at[1 + side, span]
        return pltpu.make_async_remote_copy(
            src_ref=src,
            dst_ref=fields[stage].at[dst_plane, span],
            send_sem=px_send.at[stage, side, chunk],
            recv_sem=px_recv.at[stage, side, chunk],
            device_id=(px - 1 if side == 0 else px + 1, vx),
            device_id_type=MESH,
        )

    def px_start(stage, chunk):
        @pl.when(has_left)
        def _():
            px_copy(stage, 0, chunk).start()

        @pl.when(has_right)
        def _():
            px_copy(stage, 1, chunk).start()

    def px_wait_send(stage, chunk):
        @pl.when(has_left)
        def _():
            px_copy(stage, 0, chunk).wait_send()

        @pl.when(has_right)
        def _():
            px_copy(stage, 1, chunk).wait_send()

    def px_wait_recv(stage, chunk):
        @pl.when(has_left)
        def _():
            px_copy(stage, 1, chunk).wait_recv()

        @pl.when(has_right)
        def _():
            px_copy(stage, 0, chunk).wait_recv()

    def vx_copy(stage, side):
        src_row = 1 if side == 0 else rows
        dst_row = rows + 1 if side == 0 else 0
        if stage == 0:
            src = value.at[:, pl.ds(src_row - 1, 1)]
        else:
            src = fields[stage].at[pl.ds(1, 2), pl.ds(src_row, 1)]
        return pltpu.make_async_remote_copy(
            src_ref=src,
            dst_ref=fields[stage].at[pl.ds(1, 2), pl.ds(dst_row, 1)],
            send_sem=vx_send.at[stage, side],
            recv_sem=vx_recv.at[stage, side],
            device_id=(px, vx - 1 if side == 0 else vx + 1),
            device_id_type=MESH,
        )

    def vx_start(stage):
        @pl.when(has_down)
        def _():
            vx_copy(stage, 0).start()

        @pl.when(has_up)
        def _():
            vx_copy(stage, 1).start()

    def vx_wait(stage):
        @pl.when(has_down)
        def _():
            vx_copy(stage, 0).wait_send()
            vx_copy(stage, 1).wait_recv()

        @pl.when(has_up)
        def _():
            vx_copy(stage, 1).wait_send()
            vx_copy(stage, 0).wait_recv()

    def chunk_order(index):
        return (index + chunks - 1) % chunks

    vx_start(0)

    @pl.loop(0, chunks)
    def _(index):
        px_start(0, chunk_order(index))

    load_cost.start()
    load_a2.start()

    sub = lax.broadcasted_iota(jnp.int32, (8, 128), 0)
    lane = lax.broadcasted_iota(jnp.int32, (8, 128), 1)
    sub_first, sub_last = sub == 0, sub == 7
    lane_first, lane_last = lane == 0, lane == 127

    load_a2.wait()
    a2_peak = jnp.max(jnp.abs(a2[...]), keepdims=True)
    a1_peak = jnp.max(jnp.abs(a1_v[...]), keepdims=True)
    load_value.wait()

    def ring_copy(stage, hop, axis, step, which, slot, send_slot):
        return pltpu.make_async_remote_copy(
            src_ref=red_s.at[stage, hop],
            dst_ref=red_r.at[stage, hop, slot],
            send_sem=red_send.at[stage, hop, send_slot],
            recv_sem=red_recv.at[stage, hop, slot],
            device_id=ring_device(axis, step, which),
            device_id_type=MESH,
        )

    def pair_copy(stage):
        return pltpu.make_async_remote_copy(
            src_ref=red_s.at[stage, 0],
            dst_ref=red_r.at[stage, 0, 0],
            send_sem=red_send.at[stage, 0, 0],
            recv_sem=red_recv.at[stage, 0, 0],
            device_id=partner,
            device_id_type=MESH,
        )

    axes = ("y", "z", "x")

    def all_max(stage, mine):
        red_s[stage, 0] = mine
        pair_copy(stage).start()
        pair_copy(stage).wait_recv()
        best = jnp.maximum(red_s[stage, 0], red_r[stage, 0, 0])
        for hop, axis in enumerate(axes, 1):
            red_s[stage, hop] = best

            @pl.when(core == 0)
            def _():
                for which in (0, 1):
                    ring_copy(stage, hop, axis, 1, which, 0, which).start()
                for which in (0, 1):
                    ring_copy(stage, hop, axis, 2, which, 1, 2 + which).start()

            @pl.when(core == 1)
            def _():
                for which in (0, 1):
                    ring_copy(stage, hop, axis, RING - 1, which, 2, which).start()

            for slot in range(3):
                ring_copy(stage, hop, axis, 1, 0, slot, 0).wait_recv()
            best = jnp.maximum(
                jnp.maximum(red_s[stage, hop], red_r[stage, hop, 0]),
                jnp.maximum(red_r[stage, hop, 1], red_r[stage, hop, 2]),
            )
        return best

    def all_max_drain(stage):
        pair_copy(stage).wait_send()
        for hop, axis in enumerate(axes, 1):

            @pl.when(core == 0)
            def _():
                for which in (0, 1):
                    ring_copy(stage, hop, axis, 1, which, 0, which).wait_send()
                    ring_copy(stage, hop, axis, 2, which, 1, 2 + which).wait_send()

            @pl.when(core == 1)
            def _():
                for which in (0, 1):
                    ring_copy(stage, hop, axis, RING - 1, which, 2, which).wait_send()

    def row_neighbours(row):
        here = row + 1
        down = row + first_v * ((rows - 1 - row) // (rows - 1))
        up = row + 2 - last_v * (row // (rows - 1))
        return here, down, up

    def tile(s, c):
        return pl.ds(8 * s, 8), pl.ds(128 * c, 128)

    def local_maxima(field):
        def body(row, carry):
            here, down, up = row_neighbours(row)
            m2, m3 = carry
            for plane in (1, 2):
                for c in range(tiles):
                    cells = [field[(plane, here) + tile(s, c)] for s in range(strips)]
                    turned = [pltpu.roll(x, 6, 0) for x in cells]
                    for s in range(strips):
                        above = field[(plane, up) + tile(s, c)]
                        below = field[(plane, down) + tile(s, c)]
                        m2 = jnp.maximum(m2, jnp.abs(above - below))
                        if s < strips - 1:
                            ahead = jnp.where(sub >= 6, turned[s + 1], turned[s])
                        else:
                            ahead = jnp.where(sub >= 6, cells[s], turned[s])
                        m3 = jnp.maximum(m3, jnp.abs(ahead - cells[s]))
                    step = jnp.abs(pltpu.roll(cells[0], 7, 0) - cells[0])
                    m3 = jnp.maximum(m3, jnp.where(sub_first, step, 0.0))
                    step = jnp.abs(pltpu.roll(cells[-1], 7, 0) - cells[-1])
                    m3 = jnp.maximum(m3, jnp.where(sub == 6, step, 0.0))
            return m2, m3

        zero = jnp.zeros((8, 128), jnp.float32)
        m2, m3 = lax.fori_loop(0, rows, body, (zero, zero))
        return jnp.max(m2, keepdims=True), jnp.max(m3, keepdims=True)

    def spread(x):
        return jnp.broadcast_to(x, (8, 128))

    def make_coefficients(stage, best):
        m2, m3 = spread(best[0:1]), spread(best[1:2])
        push_limit = spread(best[2:3])
        if stage == 0:
            coef[7] = push_limit
        else:
            push_limit = coef[7]
        r2 = push_limit + (DISTURBANCE) + m2 * (1.0 / (2.0 * h2 * CONTROL_COST))
        r3 = (
            spread(a2_peak) + (DISTURBANCE) + m3 * (1.0 / (2.0 * h3 * CONTROL_COST))
        )
        courant = r1 / h1 + r2 / h2 + r3 / h3 + r4 / h1
        if stage % 2 == 0:
            dt = COURANT / courant
            coef[6] = dt
            centre = 1.0 + dt * courant
            scale = dt
        else:
            dt = coef[6]
            centre = 0.5 + 0.5 * (dt * courant)
            scale = 0.5 * dt
        k1 = scale * (1.0 / (2.0 * h1))
        k2 = scale * (1.0 / (2.0 * h2))
        k3 = scale * (1.0 / (2.0 * h3))
        coef[0] = k1
        coef[1] = k2
        coef[2] = k2 * r2
        coef[3] = k3 * (1.0 / (4.0 * h3 * CONTROL_COST))
        coef[4] = k3 * r3
        coef[5] = centre
        for s in range(strips):
            speed = (
                (2 * (sub + 8 * s) + 1 - tall).astype(jnp.float32)
                * (VELOCITY_LIMIT / tall)
            )
            tab_v[0, pl.ds(8 * s, 8)] = k1 * (speed + PLANNER_SPEED)
            tab_v[1, pl.ds(8 * s, 8)] = k1 * (speed - PLANNER_SPEED)
            for c in range(tiles):
                push = a2[tile(s, c)]
                tab_a[(0,) + tile(s, c)] = k3 * (push + DISTURBANCE)
                tab_a[(1,) + tile(s, c)] = k3 * (push - DISTURBANCE)

    def update_row(stage, row):
        field = fields[stage]
        here, down, up = row_neighbours(row)
        k1, k2 = coef[0], coef[1]
        e1, e4 = k1 * r1, k1 * r4
        q2 = k2 * (1.0 / (4.0 * h2 * CONTROL_COST))
        e2, q3, e3, centre = coef[2], coef[3], coef[4], coef[5]
        speed = (2 * (vx * rows + row) + 1 - total_vx).astype(jnp.float32) * (
            VELOCITY_LIMIT / total_vx
        )
        p1 = k1 * (speed + PLANNER_SPEED)
        n1 = k1 * (speed - PLANNER_SPEED)
        for plane in (1, 2):
            left = plane_low if plane == 1 else 1
            right = 2 if plane == 1 else plane_high
            push = a1_s[plane - 1, row]
            p2 = k2 * (push + DISTURBANCE)
            n2 = k2 * (push - DISTURBANCE)
            cells, ahead, behind = {}, {}, {}

            def fetch(s):
                for c in range(tiles):
                    x = field[(plane, here) + tile(s, c)]
                    cells[s, c] = x
                    ahead[s, c] = pltpu.roll(x, 7, 0)
                    behind[s, c] = pltpu.roll(x, 1, 0)

            fetch(0)
            for s in range(strips):
                if s + 1 < strips:
                    fetch(s + 1)
                lefts = [pltpu.roll(cells[s, c], 1, 1) for c in range(tiles)]
                rights = [pltpu.roll(cells[s, c], 127, 1) for c in range(tiles)]
                v_plus = tab_v[0, pl.ds(8 * s, 8)]
                v_minus = tab_v[1, pl.ds(8 * s, 8)]
                for c in range(tiles):
                    x = cells[s, c]
                    hi = field[(right, here) + tile(s, c)]
                    lo = field[(left, here) + tile(s, c)]
                    d = hi - lo
                    total = jnp.maximum(d * p1, d * n1) - e1 * (hi + lo)
                    hi = jnp.where(
                        lane_last, rights[c + 1] if c + 1 < tiles else x, rights[c]
                    )
                    lo = jnp.where(lane_first, lefts[c - 1] if c > 0 else x, lefts[c])
                    d = hi - lo
                    total += jnp.maximum(d * v_plus, d * v_minus) - e4 * (hi + lo)
                    hi = field[(plane, up) + tile(s, c)]
                    lo = field[(plane, down) + tile(s, c)]
                    d = hi - lo
                    total += d * (jnp.where(d > 0, p2, n2) - q2 * d) - e2 * (hi + lo)
                    hi = jnp.where(
                        sub_last,
                        ahead[s + 1, c] if s + 1 < strips else x,
                        ahead[s, c],
                    )
                    lo = jnp.where(
                        sub_first, behind[s - 1, c] if s > 0 else x, behind[s, c]
                    )
                    d = hi - lo
                    p3 = tab_a[(0,) + tile(s, c)]
                    n3 = tab_a[(1,) + tile(s, c)]
                    total += d * (jnp.where(d > 0, p3, n3) - q3 * d) - e3 * (hi + lo)
                    moved = centre * x + total
                    floor = cost[(plane - 1, row) + tile(s, c)]
                    if stage % 2 == 1:
                        base = fields[stage - 1][(plane, here) + tile(s, c)]
                        moved = 0.5 * base + moved
                    result = jnp.maximum(floor, moved)
                    if stage == 3:
                        out[(plane - 1, row) + tile(s, c)] = result
                        slot = plane - 1, slice(None), pl.ds(128 * c, 128)
                        fun_s[slot] = jnp.minimum(fun_s[slot], result)
                    else:
                        fields[stage + 1][(plane, here) + tile(s, c)] = result

    fun_s[...] = jnp.full(fun_s.shape, jnp.inf, jnp.float32)

    for stage in range(4):
        vx_wait(stage)
        m2, m3 = local_maxima(fields[stage])
        mine = jnp.where(sub == 0, spread(m2), jnp.where(sub == 1, spread(m3), spread(a1_peak)))
        best = all_max(stage, mine)
        make_coefficients(stage, best)
        if stage == 0:
            load_cost.wait()

        @pl.loop(0, chunks)
        def _(index):
            chunk = chunk_order(index)
            px_wait_recv(stage, chunk)
            if stage > 0:
                px_wait_send(stage - 1, chunk)

            @pl.loop(0, CHUNK)
            def _(k):
                update_row(stage, chunk * CHUNK + k)

            if stage < 3:

                @pl.when(index > 0)
                def _():
                    px_start(stage + 1, chunk_order(index - 1))

        if stage < 3:
            px_start(stage + 1, chunk_order(chunks - 1))
            vx_start(stage + 1)
        all_max_drain(stage)

    def funnel_copy(step):
        return pltpu.make_async_remote_copy(
            src_ref=fun_s,
            dst_ref=fun_r.at[step - 1],
            send_sem=fun_send.at[step - 1],
            recv_sem=fun_recv.at[step - 1],
            device_id=(px, (vx + step) % nvx),
            device_id_type=MESH,
        )

    for step in range(1, RING):
        funnel_copy(step).start()

    @pl.loop(0, chunks)
    def _(index):
        px_wait_send(3, index)

    least = fun_s[...]
    for step in range(1, RING):
        funnel_copy(step).wait_recv()
        least = jnp.minimum(least, fun_r[step - 1])
    funnel[...] = jnp.min(least, axis=1)
    for step in range(1, RING):
        funnel_copy(step).wait_send()


def per_device(value_field, cost_field, accel_first, accel_second):
    cells_x, rows, tall, wide = value_field.shape
    field = pltpu.VMEM((cells_x + 2, rows + 2, tall, wide), jnp.float32)
    chunks = rows // CHUNK
    dma = pltpu.SemaphoreType.DMA
    hbm = pl.BlockSpec(memory_space=pl.ANY)
    vmem = pl.BlockSpec(memory_space=pltpu.VMEM)
    return pl.pallas_call(
        kernel,
        out_shape=(
            pltpu.VMEM(value_field.shape, jnp.float32),
            pltpu.VMEM((cells_x, wide), jnp.float32),
        ),
        in_specs=[pl.BlockSpec(memory_space=pltpu.SMEM), vmem, hbm, hbm, hbm],
        out_specs=(vmem, vmem),
        scratch_shapes=[
            field,
            field,
            field,
            field,
            pltpu.VMEM((cells_x, rows, tall, wide), jnp.float32),
            pltpu.VMEM((tall, wide), jnp.float32),
            pltpu.VMEM((2, tall, 128), jnp.float32),
            pltpu.VMEM((2, tall, wide), jnp.float32),
            pltpu.VMEM((4, 4, 8, 128), jnp.float32),
            pltpu.VMEM((4, 4, 3, 8, 128), jnp.float32),
            pltpu.VMEM((8, 8, 128), jnp.float32),
            pltpu.VMEM((cells_x, 8, wide), jnp.float32),
            pltpu.VMEM((RING - 1, cells_x, 8, wide), jnp.float32),
            dma((4, 2, chunks)),
            dma((4, 2, chunks)),
            dma((4, 2)),
            dma((4, 2)),
            dma((4, 4, 4)),
            dma((4, 4, 3)),
            dma((RING - 1,)),
            dma((RING - 1,)),
            dma((3,)),
        ],
        compiler_params=pltpu.CompilerParams(
            collective_id=0, has_side_effects=True, vmem_limit_bytes=56 * 1000 * 1000
        ),
    )(accel_first, accel_first, value_field, cost_field, accel_second)


def solution(mesh):
    placed = (P("px", "vx", None, None), P("px", "vx", None, None), P("px", "vx"), P())
    return jax.shard_map(
        per_device,
        mesh=mesh,
        in_specs=placed,
        out_specs=(P("px", "vx", None, None), P("px", None)),
        check_vma=False,
    )
```

time: 643 us -> 149 us (0.23); the launches traced: 635 us -> 149 us
  blocking collectives: 283 us -> 0 us
  other arithmetic: 157 us -> 0 us
  Pallas kernels: 0 us -> 145 us
  waiting for transfers between devices: 138 us -> 0 us
  starting transfers between devices: 35.4 us -> 0 us
  local copies, waits for them, and re-layouts: 14.1 us -> 2.77 us
  between operations: 7.74 us -> 0.64 us
    pmax x4 -> x0, blocking collectives: 275 us -> none  [bound_speeds(): lax.pmax((jnp.max(jnp.abs(gradient_vx)), jnp.max(jnp.abs(gradient_vy))),...]
    pallas_call x0 -> x1, Pallas kernels: none -> 145 us  [per_device(): pl.pallas_call(kernel, out_shape=(pltpu.VMEM(value_field.shape, jnp.float...]
    ppermute x16 -> x0, waiting for transfers between devices: 138 us -> none  [the longest x8 107 us: padded_2(): lax.ppermute(tail, axis, [(i, (i + 1) % count) for i in range(ends)])]
    max x3 -> x0, other arithmetic: 74.1 us -> none  [the longest x2 48.8 us: per_device(): middle = jnp.maximum(cost_field, center + step_size * change)]
    ppermute x16 -> x0, starting transfers between devices: 35.4 us -> none  [the longest x8 22.4 us: padded_2(): lax.ppermute(tail, axis, [(i, (i + 1) % count) for i in range(ends)])]
    select_n x8 -> x0, other arithmetic: 29.7 us -> none  [fill_edges(): jnp.where(jnp.logical_and(is_last, position >= count - width), high_edge,...]
    reduce_min x1 -> x0, other arithmetic: 26.4 us -> none  [per_device(): funnel_local = jnp.min(current, axis=(1, 2))]
    reduce_max x4 -> x0, other arithmetic: 18.6 us -> none  [bound_speeds(): jnp.max(jnp.abs(gradient_vx))]
  transfers between devices with their start and end apart: 16 -> 0, of which waited for: 16 -> 0; matrix products, arithmetic and copies ran while one was open for 1% -> 0% of each run, Pallas kernels for 0% -> 0%
where the time goes in v1:
time: 149 us
  Pallas kernels  145 us (97%)
  local copies, waits for them, and re-layouts  2.77 us (2%)
    pallas_call x1, Pallas kernels, per_device(): pl.pallas_call(kernel, out_shape=(pltpu.VMEM(value_field.shape, jnp.float...  145 us

profile of v1, /device:TPU:1, one launch (start us, length us, event | category | flops | bytes accessed | tf_op | source)
XLA Modules:
  0.0 148.7 jit_solution(2706182700962245697)
XLA Ops:
  0.6 145.2 %shard_map.59 = (f32[2,24,64,384]{3,2,1,0:T(8,128)S(1)}, f32[2,384]{1,0:T(2,128)S(1)}) custom-call(f32[2,24]{1,0:T(2,128)} %a1_v.1, f32[2,24]{1,0:T(2,128)} %a1_v.1, f32[2,24,64,384]{3,2,1,0:T(8,128)} %value.1, f32[2,24,64,384]{3,2,1,0:T(8,128)} %cost_hbm.1, f32[64,384]{1,0:T(8,128)} %a2_hbm.1), custom_call_target="tpu_custom_call" | custom-call | tf_op jit(solution)/shard_map/pallas_call | solution.py:510
  145.9 2.2 %copy.8 = f32[2,24,64,384]{3,2,1,0:T(8,128)} copy(f32[2,24,64,384]{3,2,1,0:T(8,128)S(1)} %get-tuple-element.2) | data formatting | bytes 9437184
  148.1 0.6 copy.9

commit v2 on v1

--- a/solution.py
+++ b/solution.py
@@ -13,7 +13,7 @@
 DISTURBANCE = 0.2
 CONTROL_COST = 1.0
 COURANT = 0.5
-CHUNK = 1
+CHUNK = 2
 RING = 4
 
 
@@ -35,6 +35,7 @@
     tab_a,
     red_s,
     red_r,
+    peak,
     coef,
     fun_s,
     fun_r,
@@ -76,12 +77,20 @@
     plane_low = first_p
     plane_high = 3 - last_p
 
-    def ring_device(axis, step, which):
-        if axis == "z":
-            return (((chip_z + step) % RING * RING + chip_x) * 2 + which, vx)
-        if axis == "x":
-            return ((chip_z * RING + (chip_x + step) % RING) * 2 + which, vx)
-        return ((chip_z * RING + chip_x) * 2 + which, (vx + step) % RING)
+    def chip_device(x, y, z, which):
+        return ((z * RING + x) * 2 + which, y)
+
+    def across(which):
+        return chip_device(chip_x + 1 - 2 * (chip_x % 2), vx, chip_z, which)
+
+    def mirror(which):
+        return chip_device(RING - 1 - chip_x, vx, chip_z, which)
+
+    def along_y(step, which):
+        return chip_device(chip_x, (vx + step) % RING, chip_z, which)
+
+    def along_z(step):
+        return chip_device(chip_x, vx, (chip_z + step) % RING, core)
 
     partner = (px + 1 - 2 * core, vx)
 
@@ -98,10 +107,13 @@
         pl.semaphore_signal(barrier, inc=1, device_id=device, device_id_type=MESH)
 
     greet(partner)
-    for axis in ("x", "y", "z"):
-        for step in range(1, RING):
-            for which in (0, 1):
-                greet(ring_device(axis, step, which))
+    for which in (0, 1):
+        greet(across(which))
+        greet(mirror(which))
+    for step in range(1, RING):
+        greet(along_y(step, 0))
+        greet(along_y(step, 1))
+        greet(along_z(step))
     far_left = jnp.logical_and(jnp.logical_and(core == 0, chip_x == 0), has_left)
     far_right = jnp.logical_and(
         jnp.logical_and(core == 1, chip_x == RING - 1), has_right
@@ -116,7 +128,7 @@
         greet((px + 1, vx))
 
     far = far_left.astype(jnp.int32) + far_right.astype(jnp.int32)
-    pl.semaphore_wait(barrier, 1 + 3 * 2 * (RING - 1) + far)
+    pl.semaphore_wait(barrier, 5 + 3 * (RING - 1) + far)
 
     def px_copy(stage, side, chunk):
         dst_plane = 3 if side == 0 else 0
@@ -177,14 +189,10 @@
             device_id_type=MESH,
         )
 
-    def vx_start(stage):
-        @pl.when(has_down)
-        def _():
-            vx_copy(stage, 0).start()
-
-        @pl.when(has_up)
-        def _():
-            vx_copy(stage, 1).start()
+    def vx_start(stage, side):
+        @pl.when(has_down if side == 0 else has_up)
+        def _():
+            vx_copy(stage, side).start()
 
     def vx_wait(stage):
         @pl.when(has_down)
@@ -200,7 +208,8 @@
     def chunk_order(index):
         return (index + chunks - 1) % chunks
 
-    vx_start(0)
+    vx_start(0, 0)
+    vx_start(0, 1)
 
     @pl.loop(0, chunks)
     def _(index):
@@ -219,70 +228,105 @@
     a1_peak = jnp.max(jnp.abs(a1_v[...]), keepdims=True)
     load_value.wait()
 
-    def ring_copy(stage, hop, axis, step, which, slot, send_slot):
+    inner = jnp.logical_or(chip_x == 1, chip_x == 2)
+    outer = jnp.logical_not(inner)
+
+    def red_copy(stage, level, slot, sent, device):
         return pltpu.make_async_remote_copy(
-            src_ref=red_s.at[stage, hop],
-            dst_ref=red_r.at[stage, hop, slot],
-            send_sem=red_send.at[stage, hop, send_slot],
-            recv_sem=red_recv.at[stage, hop, slot],
-            device_id=ring_device(axis, step, which),
+            src_ref=red_s.at[stage, level],
+            dst_ref=red_r.at[stage, slot],
+            send_sem=red_send.at[stage, sent],
+            recv_sem=red_recv.at[stage, slot],
+            device_id=device,
             device_id_type=MESH,
         )
 
-    def pair_copy(stage):
-        return pltpu.make_async_remote_copy(
-            src_ref=red_s.at[stage, 0],
-            dst_ref=red_r.at[stage, 0, 0],
-            send_sem=red_send.at[stage, 0, 0],
-            recv_sem=red_recv.at[stage, 0, 0],
-            device_id=partner,
-            device_id_type=MESH,
-        )
-
-    axes = ("y", "z", "x")
+    def y_copies(stage):
+        copies = [red_copy(stage, 0, 6, 6, partner)]
+        for step in range(1, RING):
+            for which in (0, 1):
+                n = 2 * (step - 1)
+                copies.append(
+                    red_copy(stage, 0, n + core, n + which, along_y(step, which))
+                )
+        return copies
+
+    def in_copies(stage):
+        return [red_copy(stage, 1, 7, 7 + which, across(which)) for which in (0, 1)]
+
+    def z_copies(stage):
+        return [
+            red_copy(stage, 2, 7 + step, 8 + step, along_z(step))
+            for step in range(1, RING)
+        ]
+
+    def mirror_copies(stage):
+        return [red_copy(stage, 3, 11, 12 + which, mirror(which)) for which in (0, 1)]
+
+    def out_copies(stage):
+        return [red_copy(stage, 4, 12, 14 + which, across(which)) for which in (0, 1)]
+
+    sends_in = jnp.logical_and(outer, core == chip_x // 2)
+    sends_mirror = jnp.logical_and(inner, core == chip_x // 2)
+    sends_out = jnp.logical_and(inner, core == 1 - chip_x // 2)
+
+    def start_all(copies):
+        for copy in copies:
+            copy.start()
+
+    def take(stage, best, first, last):
+        for slot in range(first, last):
+            red_copy(stage, 0, slot, 0, partner).wait_recv()
+            best = jnp.maximum(best, red_r[stage, slot])
+        return best
 
     def all_max(stage, mine):
         red_s[stage, 0] = mine
-        pair_copy(stage).start()
-        pair_copy(stage).wait_recv()
-        best = jnp.maximum(red_s[stage, 0], red_r[stage, 0, 0])
-        for hop, axis in enumerate(axes, 1):
-            red_s[stage, hop] = best
-
-            @pl.when(core == 0)
+        start_all(y_copies(stage))
+        red_s[stage, 1] = take(stage, mine, 0, 7)
+
+        @pl.when(sends_in)
+        def _():
+            start_all(in_copies(stage))
+
+        @pl.when(inner)
+        def _():
+            best = take(stage, red_s[stage, 1], 7, 8)
+            red_s[stage, 2] = best
+            start_all(z_copies(stage))
+            best = take(stage, best, 8, 11)
+            red_s[stage, 3] = best
+
+            @pl.when(sends_mirror)
             def _():
-                for which in (0, 1):
-                    ring_copy(stage, hop, axis, 1, which, 0, which).start()
-                for which in (0, 1):
-                    ring_copy(stage, hop, axis, 2, which, 1, 2 + which).start()
-
-            @pl.when(core == 1)
+                start_all(mirror_copies(stage))
+
+            red_s[stage, 4] = take(stage, best, 11, 12)
+
+            @pl.when(sends_out)
             def _():
-                for which in (0, 1):
-                    ring_copy(stage, hop, axis, RING - 1, which, 2, which).start()
-
-            for slot in range(3):
-                ring_copy(stage, hop, axis, 1, 0, slot, 0).wait_recv()
-            best = jnp.maximum(
-                jnp.maximum(red_s[stage, hop], red_r[stage, hop, 0]),
-                jnp.maximum(red_r[stage, hop, 1], red_r[stage, hop, 2]),
-            )
-        return best
+                start_all(out_copies(stage))
+
+        @pl.when(outer)
+        def _():
+            red_s[stage, 4] = take(stage, red_s[stage, 1], 12, 13)
+
+        return red_s[stage, 4]
 
     def all_max_drain(stage):
-        pair_copy(stage).wait_send()
-        for hop, axis in enumerate(axes, 1):
-
-            @pl.when(core == 0)
+        for copy in y_copies(stage):
+            copy.wait_send()
+        for copies, sends in (
+            (in_copies, sends_in),
+            (z_copies, inner),
+            (mirror_copies, sends_mirror),
+            (out_copies, sends_out),
+        ):
+
+            @pl.when(sends)
             def _():
-                for which in (0, 1):
-                    ring_copy(stage, hop, axis, 1, which, 0, which).wait_send()
-                    ring_copy(stage, hop, axis, 2, which, 1, 2 + which).wait_send()
-
-            @pl.when(core == 1)
-            def _():
-                for which in (0, 1):
-                    ring_copy(stage, hop, axis, RING - 1, which, 2, which).wait_send()
+                for copy in copies(stage):
+                    copy.wait_send()
 
     def row_neighbours(row):
         here = row + 1
@@ -293,32 +337,36 @@
     def tile(s, c):
         return pl.ds(8 * s, 8), pl.ds(128 * c, 128)
 
-    def local_maxima(field):
+    def row_maxima(field, row, carry):
+        here, down, up = row_neighbours(row)
+        m2, m3 = carry
+        for plane in (1, 2):
+            for c in range(tiles):
+                cells = [field[(plane, here) + tile(s, c)] for s in range(strips)]
+                turned = [pltpu.roll(x, 6, 0) for x in cells]
+                for s in range(strips):
+                    above = field[(plane, up) + tile(s, c)]
+                    below = field[(plane, down) + tile(s, c)]
+                    m2 = jnp.maximum(m2, jnp.abs(above - below))
+                    if s < strips - 1:
+                        ahead = jnp.where(sub >= 6, turned[s + 1], turned[s])
+                    else:
+                        ahead = jnp.where(sub >= 6, cells[s], turned[s])
+                    m3 = jnp.maximum(m3, jnp.abs(ahead - cells[s]))
+                step = jnp.abs(pltpu.roll(cells[0], 7, 0) - cells[0])
+                m3 = jnp.maximum(m3, jnp.where(sub_first, step, 0.0))
+                step = jnp.abs(pltpu.roll(cells[-1], 7, 0) - cells[-1])
+                m3 = jnp.maximum(m3, jnp.where(sub == 6, step, 0.0))
+        return m2, m3
+
+    def add_maxima(field, first, last):
         def body(row, carry):
-            here, down, up = row_neighbours(row)
-            m2, m3 = carry
-            for plane in (1, 2):
-                for c in range(tiles):
-                    cells = [field[(plane, here) + tile(s, c)] for s in range(strips)]
-                    turned = [pltpu.roll(x, 6, 0) for x in cells]
-                    for s in range(strips):
-                        above = field[(plane, up) + tile(s, c)]
-                        below = field[(plane, down) + tile(s, c)]
-                        m2 = jnp.maximum(m2, jnp.abs(above - below))
-                        if s < strips - 1:
-                            ahead = jnp.where(sub >= 6, turned[s + 1], turned[s])
-                        else:
-                            ahead = jnp.where(sub >= 6, cells[s], turned[s])
-                        m3 = jnp.maximum(m3, jnp.abs(ahead - cells[s]))
-                    step = jnp.abs(pltpu.roll(cells[0], 7, 0) - cells[0])
-                    m3 = jnp.maximum(m3, jnp.where(sub_first, step, 0.0))
-                    step = jnp.abs(pltpu.roll(cells[-1], 7, 0) - cells[-1])
-                    m3 = jnp.maximum(m3, jnp.where(sub == 6, step, 0.0))
-            return m2, m3
-
-        zero = jnp.zeros((8, 128), jnp.float32)
-        m2, m3 = lax.fori_loop(0, rows, body, (zero, zero))
-        return jnp.max(m2, keepdims=True), jnp.max(m3, keepdims=True)
+            return row_maxima(field, row, carry)
+
+        peak[0], peak[1] = lax.fori_loop(first, last, body, (peak[0], peak[1]))
+
+    def clear_maxima():
+        peak[...] = jnp.zeros(peak.shape, jnp.float32)
 
     def spread(x):
         return jnp.broadcast_to(x, (8, 128))
@@ -443,12 +491,21 @@
 
     fun_s[...] = jnp.full(fun_s.shape, jnp.inf, jnp.float32)
 
+    near_end = rows - CHUNK - 1
+    clear_maxima()
+    add_maxima(f0, 1, near_end)
     for stage in range(4):
+        field = fields[stage]
+        add_maxima(field, near_end, rows - 1)
         vx_wait(stage)
-        m2, m3 = local_maxima(fields[stage])
-        mine = jnp.where(sub == 0, spread(m2), jnp.where(sub == 1, spread(m3), spread(a1_peak)))
+        add_maxima(field, 0, 1)
+        add_maxima(field, rows - 1, rows)
+        m2 = spread(jnp.max(peak[0], keepdims=True))
+        m3 = spread(jnp.max(peak[1], keepdims=True))
+        mine = jnp.where(sub == 0, m2, jnp.where(sub == 1, m3, spread(a1_peak)))
         best = all_max(stage, mine)
         make_coefficients(stage, best)
+        clear_maxima()
         if stage == 0:
             load_cost.wait()
 
@@ -469,9 +526,24 @@
                 def _():
                     px_start(stage + 1, chunk_order(index - 1))
 
+                @pl.when(index == 1)
+                def _():
+                    vx_start(stage + 1, 1)
+
+                @pl.when(index == 2)
+                def _():
+                    vx_start(stage + 1, 0)
+                    if CHUNK > 1:
+                        add_maxima(fields[stage + 1], 1, 2 * CHUNK - 1)
+
+                @pl.when(index > 2)
+                def _():
+                    add_maxima(
+                        fields[stage + 1], chunk * CHUNK - 1, chunk * CHUNK + CHUNK - 1
+                    )
+
         if stage < 3:
             px_start(stage + 1, chunk_order(chunks - 1))
-            vx_start(stage + 1)
         all_max_drain(stage)
 
     def funnel_copy(step):
@@ -524,8 +596,9 @@
             pltpu.VMEM((tall, wide), jnp.float32),
             pltpu.VMEM((2, tall, 128), jnp.float32),
             pltpu.VMEM((2, tall, wide), jnp.float32),
-            pltpu.VMEM((4, 4, 8, 128), jnp.float32),
-            pltpu.VMEM((4, 4, 3, 8, 128), jnp.float32),
+            pltpu.VMEM((4, 5, 8, 128), jnp.float32),
+            pltpu.VMEM((4, 13, 8, 128), jnp.float32),
+            pltpu.VMEM((2, 8, 128), jnp.float32),
             pltpu.VMEM((8, 8, 128), jnp.float32),
             pltpu.VMEM((cells_x, 8, wide), jnp.float32),
             pltpu.VMEM((RING - 1, cells_x, 8, wide), jnp.float32),
@@ -533,8 +606,8 @@
             dma((4, 2, chunks)),
             dma((4, 2)),
             dma((4, 2)),
-            dma((4, 4, 4)),
-            dma((4, 4, 3)),
+            dma((4, 16)),
+            dma((4, 13)),
             dma((RING - 1,)),
             dma((RING - 1,)),
             dma((3,)),

time: 149 us -> 122 us (0.82)
  Pallas kernels: 145 us -> 119 us
    pallas_call x1, Pallas kernels: 145 us -> 119 us  [per_device(): pl.pallas_call(kernel, out_shape=(pltpu.VMEM(value_field.shape, jnp.float...]
where the time goes in v2:
time: 122 us
  Pallas kernels  119 us (98%)
  local copies, waits for them, and re-layouts  2.77 us (2%)
    pallas_call x1, Pallas kernels, per_device(): pl.pallas_call(kernel, out_shape=(pltpu.VMEM(value_field.shape, jnp.float...  119 us
    unnamed x2, local copies, waits for them, and re-layouts  2.77 us

profile of v2, /device:TPU:1, one launch (start us, length us, event | category | flops | bytes accessed | tf_op | source)
XLA Modules:
  0.0 122.3 jit_solution(11132385664946231916)
XLA Ops:
  0.6 118.9 %shard_map.59 = (f32[2,24,64,384]{3,2,1,0:T(8,128)S(1)}, f32[2,384]{1,0:T(2,128)S(1)}) custom-call(f32[2,24]{1,0:T(2,128)} %a1_v.1, f32[2,24]{1,0:T(2,128)} %a1_v.1, f32[2,24,64,384]{3,2,1,0:T(8,128)} %value.1, f32[2,24,64,384]{3,2,1,0:T(8,128)} %cost_hbm.1, f32[64,384]{1,0:T(8,128)} %a2_hbm.1), custom_call_target="tpu_custom_call" | custom-call | tf_op jit(solution)/shard_map/pallas_call | solution.py:582
  119.5 2.2 %copy.8 = f32[2,24,64,384]{3,2,1,0:T(8,128)} copy(f32[2,24,64,384]{3,2,1,0:T(8,128)S(1)} %get-tuple-element.2) | data formatting | bytes 9437184
  121.7 0.6 copy.9

commit v3 on v2

--- a/solution.py
+++ b/solution.py
@@ -18,8 +18,7 @@
 
 
 def kernel(
-    a1_s,
-    a1_v,
+    a1_hbm,
     value,
     cost_hbm,
     a2_hbm,
@@ -30,6 +29,8 @@
     f2,
     f3,
     cost,
+    a1_s,
+    a1_v,
     a2,
     tab_v,
     tab_a,
@@ -37,6 +38,7 @@
     red_r,
     peak,
     coef,
+    least,
     fun_s,
     fun_r,
     px_send,
@@ -99,6 +101,8 @@
     )
     load_cost = pltpu.make_async_copy(cost_hbm, cost, load_sem.at[1])
     load_a2 = pltpu.make_async_copy(a2_hbm, a2, load_sem.at[2])
+    load_a1_s = pltpu.make_async_copy(a1_hbm, a1_s, load_sem.at[3])
+    load_a1_v = pltpu.make_async_copy(a1_hbm, a1_v, load_sem.at[4])
     load_value.start()
 
     barrier = pltpu.get_barrier_semaphore()
@@ -215,8 +219,10 @@
     def _(index):
         px_start(0, chunk_order(index))
 
+    load_a1_v.start()
+    load_a1_s.start()
+    load_a2.start()
     load_cost.start()
-    load_a2.start()
 
     sub = lax.broadcasted_iota(jnp.int32, (8, 128), 0)
     lane = lax.broadcasted_iota(jnp.int32, (8, 128), 1)
@@ -224,6 +230,8 @@
     lane_first, lane_last = lane == 0, lane == 127
 
     load_a2.wait()
+    load_a1_v.wait()
+    load_a1_s.wait()
     a2_peak = jnp.max(jnp.abs(a2[...]), keepdims=True)
     a1_peak = jnp.max(jnp.abs(a1_v[...]), keepdims=True)
     load_value.wait()
@@ -485,11 +493,11 @@
                     if stage == 3:
                         out[(plane - 1, row) + tile(s, c)] = result
                         slot = plane - 1, slice(None), pl.ds(128 * c, 128)
-                        fun_s[slot] = jnp.minimum(fun_s[slot], result)
+                        least[slot] = jnp.minimum(least[slot], result)
                     else:
                         fields[stage + 1][(plane, here) + tile(s, c)] = result
 
-    fun_s[...] = jnp.full(fun_s.shape, jnp.inf, jnp.float32)
+    least[...] = jnp.full(least.shape, jnp.inf, jnp.float32)
 
     near_end = rows - CHUNK - 1
     clear_maxima()
@@ -544,7 +552,7 @@
 
         if stage < 3:
             px_start(stage + 1, chunk_order(chunks - 1))
-        all_max_drain(stage)
+            all_max_drain(stage)
 
     def funnel_copy(step):
         return pltpu.make_async_remote_copy(
@@ -556,20 +564,40 @@
             device_id_type=MESH,
         )
 
-    for step in range(1, RING):
+    fun_s[...] = jnp.min(least[...], axis=1)
+    for step in (2, 1, 3):
         funnel_copy(step).start()
 
     @pl.loop(0, chunks)
     def _(index):
         px_wait_send(3, index)
 
-    least = fun_s[...]
+    all_max_drain(3)
+    lowest = fun_s[...]
     for step in range(1, RING):
         funnel_copy(step).wait_recv()
-        least = jnp.minimum(least, fun_r[step - 1])
-    funnel[...] = jnp.min(least, axis=1)
+        lowest = jnp.minimum(lowest, fun_r[step - 1])
+    funnel[...] = lowest
     for step in range(1, RING):
         funnel_copy(step).wait_send()
+
+
+def store_kernel(field, funnel, field_out, funnel_out, sem):
+    parts = 8
+    rows = field.shape[1] // (parts // 2)
+    copies = [
+        pltpu.make_async_copy(
+            field.at[n % 2, pl.ds(n // 2 * rows, rows)],
+            field_out.at[n % 2, pl.ds(n // 2 * rows, rows)],
+            sem.at[n],
+        )
+        for n in range(parts)
+    ]
+    copies.append(pltpu.make_async_copy(funnel, funnel_out, sem.at[parts]))
+    for copy in copies:
+        copy.start()
+    for copy in copies:
+        copy.wait()
 
 
 def per_device(value_field, cost_field, accel_first, accel_second):
@@ -579,13 +607,13 @@
     dma = pltpu.SemaphoreType.DMA
     hbm = pl.BlockSpec(memory_space=pl.ANY)
     vmem = pl.BlockSpec(memory_space=pltpu.VMEM)
-    return pl.pallas_call(
+    field_end, funnel = pl.pallas_call(
         kernel,
         out_shape=(
             pltpu.VMEM(value_field.shape, jnp.float32),
             pltpu.VMEM((cells_x, wide), jnp.float32),
         ),
-        in_specs=[pl.BlockSpec(memory_space=pltpu.SMEM), vmem, hbm, hbm, hbm],
+        in_specs=[hbm, hbm, hbm, hbm],
         out_specs=(vmem, vmem),
         scratch_shapes=[
             field,
@@ -593,6 +621,8 @@
             field,
             field,
             pltpu.VMEM((cells_x, rows, tall, wide), jnp.float32),
+            pltpu.SMEM((cells_x, rows), jnp.float32),
+            pltpu.VMEM((cells_x, rows), jnp.float32),
             pltpu.VMEM((tall, wide), jnp.float32),
             pltpu.VMEM((2, tall, 128), jnp.float32),
             pltpu.VMEM((2, tall, wide), jnp.float32),
@@ -601,7 +631,8 @@
             pltpu.VMEM((2, 8, 128), jnp.float32),
             pltpu.VMEM((8, 8, 128), jnp.float32),
             pltpu.VMEM((cells_x, 8, wide), jnp.float32),
-            pltpu.VMEM((RING - 1, cells_x, 8, wide), jnp.float32),
+            pltpu.VMEM((cells_x, wide), jnp.float32),
+            pltpu.VMEM((RING - 1, cells_x, wide), jnp.float32),
             dma((4, 2, chunks)),
             dma((4, 2, chunks)),
             dma((4, 2)),
@@ -610,12 +641,28 @@
             dma((4, 13)),
             dma((RING - 1,)),
             dma((RING - 1,)),
-            dma((3,)),
+            dma((5,)),
         ],
         compiler_params=pltpu.CompilerParams(
             collective_id=0, has_side_effects=True, vmem_limit_bytes=56 * 1000 * 1000
         ),
-    )(accel_first, accel_first, value_field, cost_field, accel_second)
+    )(accel_first, value_field, cost_field, accel_second)
+    return tuple(
+        pl.pallas_call(
+            store_kernel,
+            out_shape=(
+                jax.ShapeDtypeStruct(value_field.shape, jnp.float32),
+                jax.ShapeDtypeStruct((cells_x, wide), jnp.float32),
+            ),
+            in_specs=[vmem, vmem],
+            out_specs=(hbm, hbm),
+            scratch_shapes=[dma((9,))],
+            compiler_params=pltpu.CompilerParams(vmem_limit_bytes=1 << 20),
+        )(
+            pltpu.with_memory_space_constraint(field_end, pltpu.VMEM),
+            pltpu.with_memory_space_constraint(funnel, pltpu.VMEM),
+        )
+    )
 
 
 def solution(mesh):

time: 122 us -> 120 us (0.984)
  local copies, waits for them, and re-layouts: 2.77 us -> 0 us
    unnamed x2 -> x0, local copies, waits for them, and re-layouts: 2.77 us -> none
    pallas_call x0 -> x1, Pallas kernels: none -> 2.26 us  [per_device(): pl.pallas_call(store_kernel, out_shape=(jax.ShapeDtypeStruct(value_field....]
    pallas_call x1, Pallas kernels: 119 us -> 117 us  [per_device(): pl.pallas_call(kernel, out_shape=(pltpu.VMEM(value_field.shape, jnp.float...]
where the time goes in v3:
time: 120 us
  Pallas kernels  120 us (100%)
    pallas_call x1, Pallas kernels, per_device(): pl.pallas_call(kernel, out_shape=(pltpu.VMEM(value_field.shape, jnp.float...  117 us

profile of v3, /device:TPU:1, one launch (start us, length us, event | category | flops | bytes accessed | tf_op | source)
XLA Modules:
  0.0 120.4 jit_solution(12904026005048114215)
XLA Ops:
  0.6 117.5 %shard_map.59 = (f32[2,24,64,384]{3,2,1,0:T(8,128)S(1)}, f32[2,384]{1,0:T(2,128)S(1)}) custom-call(f32[2,24]{1,0:T(2,128)} %a1_hbm.1, f32[2,24,64,384]{3,2,1,0:T(8,128)} %value.1, f32[2,24,64,384]{3,2,1,0:T(8,128)} %cost_hbm.1, f32[64,384]{1,0:T(8,128)} %a2_hbm.1), custom_call_target="tpu_custom_call" | custom-call | tf_op jit(solution)/shard_map/pallas_call | solution.py:610
  118.1 2.3 %shard_map.60 = (f32[2,24,64,384]{3,2,1,0:T(8,128)}, f32[2,384]{1,0:T(2,128)}) custom-call(f32[2,24,64,384]{3,2,1,0:T(8,128)S(1)} %get-tuple-element.4.field, f32[2,384]{1,0:T(2,128)S(1)} %get-tuple-element.5.funnel), custom_call_target="tpu_custom_call" | custom-call | tf_op jit(solution)/shard_map/pallas_call | solution.py:651

commit v4 on v3

--- a/solution.py
+++ b/solution.py
@@ -13,7 +13,8 @@
 DISTURBANCE = 0.2
 CONTROL_COST = 1.0
 COURANT = 0.5
-CHUNK = 2
+BLOCK = 4
+SIZES = (4, 4, 4, 2)
 RING = 4
 
 
@@ -57,7 +58,6 @@
     wide = cost.shape[3]
     strips = tall // 8
     tiles = wide // 128
-    chunks = rows // CHUNK
     px, vx = lax.axis_index("px"), lax.axis_index("vx")
     npx, nvx = lax.axis_size("px"), lax.axis_size("vx")
     total_vx = rows * nvx
@@ -136,9 +136,10 @@
 
     def px_copy(stage, side, chunk):
         dst_plane = 3 if side == 0 else 0
-        span = pl.ds(chunk * CHUNK + 1, CHUNK)
+        size = SIZES[stage]
+        span = pl.ds(chunk * size + 1, size)
         if stage == 0:
-            src = value.at[side, pl.ds(chunk * CHUNK, CHUNK)]
+            src = value.at[side, pl.ds(chunk * size, size)]
         else:
             src = fields[stage].at[1 + side, span]
         return pltpu.make_async_remote_copy(
@@ -167,6 +168,11 @@
         @pl.when(has_right)
         def _():
             px_copy(stage, 1, chunk).wait_send()
+
+    def px_drain(stage):
+        @pl.loop(0, rows // SIZES[stage])
+        def _(chunk):
+            px_wait_send(stage, chunk)
 
     def px_wait_recv(stage, chunk):
         @pl.when(has_left)
@@ -209,15 +215,16 @@
             vx_copy(stage, 1).wait_send()
             vx_copy(stage, 0).wait_recv()
 
-    def chunk_order(index):
-        return (index + chunks - 1) % chunks
+    def order(index, size):
+        count = rows // size
+        return (index + count - BLOCK // size) % count
 
     vx_start(0, 0)
     vx_start(0, 1)
 
-    @pl.loop(0, chunks)
+    @pl.loop(0, rows // SIZES[0])
     def _(index):
-        px_start(0, chunk_order(index))
+        px_start(0, order(index, SIZES[0]))
 
     load_a1_v.start()
     load_a1_s.start()
@@ -499,11 +506,14 @@
 
     least[...] = jnp.full(least.shape, jnp.inf, jnp.float32)
 
-    near_end = rows - CHUNK - 1
+    near_end = rows - BLOCK - 1
     clear_maxima()
     add_maxima(f0, 1, near_end)
     for stage in range(4):
         field = fields[stage]
+        size = SIZES[stage]
+        block = BLOCK if stage < 3 else size
+        blocks = rows // block
         add_maxima(field, near_end, rows - 1)
         vx_wait(stage)
         add_maxima(field, 0, 1)
@@ -517,22 +527,26 @@
         if stage == 0:
             load_cost.wait()
 
-        @pl.loop(0, chunks)
+        def send_block(index):
+            sent = SIZES[stage + 1]
+            for k in range(block // sent):
+                px_start(stage + 1, order(index, block) * (block // sent) + k)
+
+        @pl.loop(0, blocks)
         def _(index):
-            chunk = chunk_order(index)
-            px_wait_recv(stage, chunk)
-            if stage > 0:
-                px_wait_send(stage - 1, chunk)
-
-            @pl.loop(0, CHUNK)
+            first = order(index, block) * block
+            for k in range(block // size):
+                px_wait_recv(stage, order(index, block) * (block // size) + k)
+
+            @pl.loop(0, block)
             def _(k):
-                update_row(stage, chunk * CHUNK + k)
+                update_row(stage, first + k)
 
             if stage < 3:
 
                 @pl.when(index > 0)
                 def _():
-                    px_start(stage + 1, chunk_order(index - 1))
+                    send_block(index - 1)
 
                 @pl.when(index == 1)
                 def _():
@@ -541,18 +555,17 @@
                 @pl.when(index == 2)
                 def _():
                     vx_start(stage + 1, 0)
-                    if CHUNK > 1:
-                        add_maxima(fields[stage + 1], 1, 2 * CHUNK - 1)
+                    add_maxima(fields[stage + 1], 1, 2 * block - 1)
 
                 @pl.when(index > 2)
                 def _():
-                    add_maxima(
-                        fields[stage + 1], chunk * CHUNK - 1, chunk * CHUNK + CHUNK - 1
-                    )
+                    add_maxima(fields[stage + 1], first - 1, first + block - 1)
 
         if stage < 3:
-            px_start(stage + 1, chunk_order(chunks - 1))
+            send_block(blocks - 1)
             all_max_drain(stage)
+        if stage > 0 and stage < 3:
+            px_drain(stage - 1)
 
     def funnel_copy(step):
         return pltpu.make_async_remote_copy(
@@ -568,10 +581,8 @@
     for step in (2, 1, 3):
         funnel_copy(step).start()
 
-    @pl.loop(0, chunks)
-    def _(index):
-        px_wait_send(3, index)
-
+    px_drain(2)
+    px_drain(3)
     all_max_drain(3)
     lowest = fun_s[...]
     for step in range(1, RING):
@@ -603,7 +614,7 @@
 def per_device(value_field, cost_field, accel_first, accel_second):
     cells_x, rows, tall, wide = value_field.shape
     field = pltpu.VMEM((cells_x + 2, rows + 2, tall, wide), jnp.float32)
-    chunks = rows // CHUNK
+    chunks = rows // min(SIZES)
     dma = pltpu.SemaphoreType.DMA
     hbm = pl.BlockSpec(memory_space=pl.ANY)
     vmem = pl.BlockSpec(memory_space=pltpu.VMEM)

time: 120 us -> 120 us (level)
  no operation moved by 1% of the time
where the time goes in v4:
time: 120 us
  Pallas kernels  120 us (100%)
    pallas_call x1, Pallas kernels, per_device(): pl.pallas_call(kernel, out_shape=(pltpu.VMEM(value_field.shape, jnp.float...  117 us

profile of v4, /device:TPU:1, one launch (start us, length us, event | category | flops | bytes accessed | tf_op | source)
XLA Modules:
  0.0 120.2 jit_solution(6837953584552346557)
XLA Ops:
  0.6 117.3 %shard_map.59 = (f32[2,24,64,384]{3,2,1,0:T(8,128)S(1)}, f32[2,384]{1,0:T(2,128)S(1)}) custom-call(f32[2,24]{1,0:T(2,128)} %a1_hbm.1, f32[2,24,64,384]{3,2,1,0:T(8,128)} %value.1, f32[2,24,64,384]{3,2,1,0:T(8,128)} %cost_hbm.1, f32[64,384]{1,0:T(8,128)} %a2_hbm.1), custom_call_target="tpu_custom_call" | custom-call | tf_op jit(solution)/shard_map/pallas_call | solution.py:621
  118.0 2.3 %shard_map.60 = (f32[2,24,64,384]{3,2,1,0:T(8,128)}, f32[2,384]{1,0:T(2,128)}) custom-call(f32[2,24,64,384]{3,2,1,0:T(8,128)S(1)} %get-tuple-element.4.field, f32[2,384]{1,0:T(2,128)S(1)} %get-tuple-element.5.funnel), custom_call_target="tpu_custom_call" | custom-call | tf_op jit(solution)/shard_map/pallas_call | solution.py:662
